TPU v7x, 32 devices: a whole 2x2x4 slice. The times are simulated.
32 devices in a mesh: groups: 2 (over y), rows: 4 (over z), cols: 4 (over x, core).
Axes of the slice: x: 2, y: 2, z: 4, core: 2. Of those that a mesh axis runs over, the one named last changes fastest.
Arguments:
- tokens: bfloat16 [128, 256, 512], P(('groups', 'rows'), 'cols'), parts along dimension 0, may hold values from -30 to 30
- qkv_weight: bfloat16 [512, 1536], replicated, may hold values from -0.25 to 0.25
- depth_kernel: float32 [25, 1536], replicated, may hold values from -1.25 to 1.25
- group_kernel: bfloat16 [48, 32, 32], replicated, may hold values from -1 to 1
- proj_weight: bfloat16 [1024, 512], replicated, may hold values from -0.1875 to 0.1875
- out_gain: float32 [512], replicated, may hold values from 4 to 16
- out_bias: float32 [512], replicated, may hold values from -3 to 3
Outputs:
- output: bfloat16 [128, 256, 512], P(('groups', 'rows'), 'cols'), parts along dimension 0
There are 2 independent parts, one for each index of `groups`. A program takes and returns all parts, laid end to end along the dimension named above; an argument that names none is the same for every part. Nothing has to cross between parts.
All inputs are finite; a program needn't handle non-finite values.
Results may differ from a plain program's by a relative error of at most 0.0048.
Values may be sent and summed in bfloat16 or wider, within the bound.
A program may use at most 64 MiB of HBM per device.

v0:
```python
import jax
import jax.numpy as jnp
from jax import lax
from jax.sharding import PartitionSpec as P

HEAD_DIM = 32


def padded_2(value, sides, width):
    for axis, dim in sides:
        size, length = (lax.axis_size(axis), value.shape[dim])
        up = [(i, (i + 1) % size) for i in range(size - 1)]
        down = [(j, i) for i, j in up]
        last = lax.slice_in_dim(value, length - width, length, axis=dim)
        leading = lax.slice_in_dim(value, 0, width, axis=dim)
        before = lax.ppermute(last, axis, up)
        after = lax.ppermute(leading, axis, down)
        value = jnp.concatenate([before, value, after], axis=dim)
    return value


def feature_map(inputs):
    return jax.nn.elu(inputs.astype(jnp.float32)) + 1.0


def aggregate(padded, depth_kernel, group_kernel, height, breadth):
    channels = padded.shape[2]
    summed = jnp.zeros((height, breadth, channels), jnp.float32)
    for offset_row in range(5):
        for offset_col in range(5):
            window = padded[offset_row : offset_row + height, offset_col : offset_col + breadth]
            summed = summed + window * depth_kernel[offset_row * 5 + offset_col]
    spread = summed.astype(jnp.bfloat16).reshape(height * breadth, channels // HEAD_DIM, HEAD_DIM)
    grouped = jnp.einsum("ngc,gcd->ngd", spread, group_kernel, preferred_element_type=jnp.float32)
    return grouped.astype(jnp.bfloat16).reshape(height * breadth, channels)


def context_states(source):
    amount = source.shape[0]
    grouped = source.reshape(amount, -1, 3, HEAD_DIM)
    key_feats = feature_map(grouped[:, :, 1]).astype(jnp.bfloat16)
    values = grouped[:, :, 2]
    states = jnp.einsum("nhd,nhe->hde", key_feats, values, preferred_element_type=jnp.float32)
    totals = jnp.sum(key_feats.astype(jnp.float32), axis=0)
    return (states, totals)


def body(tokens, qkv_weight, depth_kernel, group_kernel, proj_weight, out_gain, out_bias):
    height, breadth, channels = tokens.shape
    amount = height * breadth
    triple = jnp.dot(
        tokens.reshape(amount, channels), qkv_weight, preferred_element_type=jnp.float32
    )
    triple = triple.astype(jnp.bfloat16).reshape(height, breadth, 3 * channels)
    padded = padded_2(triple, (("rows", 0), ("cols", 1)), 2)
    flat_triple = triple.reshape(amount, 3 * channels)
    plain_state, plain_total = context_states(flat_triple)
    aggregated = aggregate(padded, depth_kernel, group_kernel, height, breadth)
    scaled_state, scaled_total = context_states(aggregated)
    states, totals = lax.psum(
        (
            jnp.concatenate([plain_state, scaled_state], 0),
            jnp.concatenate([plain_total, scaled_total], 0),
        ),
        ("rows", "cols"),
    )
    queries = jnp.concatenate(
        [
            feature_map(flat_triple.reshape(amount, -1, 3, HEAD_DIM)[:, :, 0]),
            feature_map(aggregated.reshape(amount, -1, 3, HEAD_DIM)[:, :, 0]),
        ],
        1,
    )
    numerator = jnp.einsum("nhd,hde->nhe", queries, states, precision=lax.Precision.HIGHEST)
    denominator = jnp.einsum("nhd,hd->nh", queries, totals, precision=lax.Precision.HIGHEST)
    attended = (
        (numerator / denominator[:, :, None]).astype(jnp.bfloat16).reshape(amount, 2 * channels)
    )
    projected = jnp.dot(attended, proj_weight, preferred_element_type=jnp.float32)
    result = tokens.reshape(amount, channels).astype(jnp.float32) + out_gain * projected + out_bias
    return result.astype(jnp.bfloat16).reshape(height, breadth, channels)


def solution(mesh):
    placed = (P(("groups", "rows"), "cols", None), P(), P(), P(), P(), P(), P())
    return jax.shard_map(
        body,
        mesh=mesh,
        in_specs=placed,
        out_specs=P(("groups", "rows"), "cols", None),
        check_vma=False,
    )
```

profile of v0, /device:TPU:1, one launch (start us, length us, event | category | flops | bytes accessed | tf_op | source)
XLA Modules:
  0.0 203.0 jit_solution(8702821918944475526)
XLA Ops:
  6.5 1.4 copy-done
  7.9 3.0 %convolution_convert_fusion = bf16[1024,1536]{1,0:T(8,128)(2,1)S(1)} fusion(bf16[1024,512]{1,0:T(8,128)(2,1)} %bitcast.85, bf16[512,1536]{1,0:T(8,128)(2,1)S(1)} %copy-done), kind=kOutput, calls=%fused_computation.14 | convolution fusion | flops 1612185600 | bytes 5767168 | tf_op jit(solution)/shard_map/dot_general | solution.py:51
  11.0 1.7 copy-done.1
  12.6 0.1 fusion.25
  12.7 4.1 %collective-permute-start = (bf16[2,64,1536]{2,1,0:T(8,128)(2,1)S(1)}, bf16[2,64,1536]{2,1,0:T(8,128)(2,1)S(1)}, u32[]{:S(2)}, u32[]{:S(2)}) collective-permute-start(bf16[2,64,1536]{2,1,0:T(8,128)(2,1)S(1)} %bitcast.82), channel_id=1, source_target_pairs={{0,4},{4,8},{8,12},{1,5},{5,9},{9,13},{2,6},{6,10},{10,14},{3,7},{... | collective-permute-start | bytes 1179656 | tf_op jit(solution)/shard_map/ppermute | solution.py:16
  16.7 1.3 collective-permute-start.1
  18.0 4.7 %copy.26 = bf16[1024,1536]{0,1:T(8,128)(2,1)} copy(bf16[1024,1536]{1,0:T(8,128)(2,1)} %copy-done.1) | data formatting | bytes 6291456 | tf_op jit(solution)/shard_map/convert_element_type | solution.py:54
  22.8 3.5 %fusion.16 = f32[16,32,32]{2,1,0:T(8,128)} fusion(bf16[1024,16,3,32]{0,3,2,1:T(8,128)(2,1)} %bitcast.77), kind=kOutput, calls=%fused_computation.45 | convolution fusion | flops 36700160 | bytes 2162688 | tf_op jit(solution)/shard_map/nhd,nhe->hde/dot_general | solution.py:43
  26.3 0.0 collective-permute-done
  26.3 2.0 %collective-permute-done.1 = bf16[2,64,1536]{2,1,0:T(8,128)(2,1)S(1)} collective-permute-done((bf16[2,64,1536]{2,1,0:T(8,128)(2,1)S(1)}, bf16[2,64,1536]{2,1,0:T(8,128)(2,1)S(1)}, u32[]{:S(2)}, u32[]{:S(2)}) %collective-permute-start.1) | collective-permute-done | bytes 393248 | tf_op jit(solution)/shard_map/ppermute | solution.py:17
  28.3 0.2 pad_maximum_fusion.11
  28.5 4.9 %collective-permute-start.2 = (bf16[20,2,1536]{2,1,0:T(2,128)(2,1)S(1)}, bf16[20,2,1536]{2,1,0:T(2,128)(2,1)S(1)}, u32[]{:S(2)}, u32[]{:S(2)}) collective-permute-start(bf16[20,2,1536]{2,1,0:T(2,128)(2,1)S(1)} %get-tuple-element.32), channel_id=1, source_target_pairs={{0,1},{1,2},{2,3},{4,5},{5,6},{6,7},{8,9},{9,10},{10,11},{12,13},{... | collective-permute-start | bytes 368648 | tf_op jit(solution)/shard_map/ppermute | solution.py:16
  33.4 2.1 %collective-permute-start.3 = (bf16[20,2,1536]{2,1,0:T(2,128)(2,1)S(1)}, bf16[20,2,1536]{2,1,0:T(2,128)(2,1)S(1)}, u32[]{:S(2)}, u32[]{:S(2)}) collective-permute-start(bf16[20,2,1536]{2,1,0:T(2,128)(2,1)S(1)} %get-tuple-element.33), channel_id=1, source_target_pairs={{1,0},{2,1},{3,2},{5,4},{6,5},{7,6},{9,8},{10,9},{11,10},{13,12},{... | collective-permute-start | bytes 368648 | tf_op jit(solution)/shard_map/ppermute | solution.py:17
  35.5 0.9 slice_reduce_fusion.24
  36.4 0.7 copy.29
  37.1 1.1 slice_reduce_fusion.23
  38.3 1.2 collective-permute-done.3
  39.6 5.1 %maximum_maximum_fusion = (bf16[20,66,1536]{2,1,0:T(8,128)(2,1)S(1)}, bf16[20,66,1536]{2,1,0:T(8,128)(2,1)S(1)}) fusion(bf16[2,64,1536]{2,1,0:T(8,128)(2,1)S(1)} %collective-permute-done.1, bf16[16,64,1536]{2,1,0:T(8,128)(2,1)} %bitcast.74, bf16[2,64,1536]{2,1,0:T(8,128)(2,1)S(1)} %collective-permute-done, ...), kind=kLoop, calls=%fused_computation.9 | loop fusion | flops 32440320 | bytes 12288000 | tf_op jit(solution)/shard_map/concatenate | solution.py:18
  44.9 24.0 %add_convert_fusion = bf16[16,64,1536]{2,1,0:T(8,128)(2,1)} fusion(bf16[16,64,1536]{2,1,0:T(8,128)(2,1)S(1)} %bitcast.76, bf16[2,64,1536]{2,1,0:T(8,128)(2,1)S(1)} %collective-permute-done.1, bf16[2,64,1536]{2,1,0:T(8,128)(2,1)S(1)} %collective-permute-done, bf16[20,66,1536]{2,1,0:T(8,128)(2,1)S(1)} %get-tuple-element.31, ...), kind=kLoop, calls=%fused_computation.8 | loop fusion | flops 124256256 | bytes 70146048 | tf_op jit(solution)/shard_map/convert_element_type | solution.py:33
  68.9 8.6 %copy.28 = bf16[16,64,1536]{1,0,2:T(8,128)(2,1)} copy(bf16[16,64,1536]{2,1,0:T(8,128)(2,1)} %add_convert_fusion) | data formatting | bytes 6291456 | tf_op jit(solution)/shard_map/convert_element_type | solution.py:33
  77.5 9.4 %reshape.56 = bf16[1024,48,32]{0,2,1:T(8,128)(2,1)} reshape(bf16[16,64,1536]{1,0,2:T(8,128)(2,1)} %copy.28) | data formatting | bytes 6291456 | tf_op jit(solution)/shard_map/reshape | solution.py:33
  86.9 2.8 %convolution_convert_fusion.1 = bf16[48,1024,32]{1,2,0:T(8,128)(2,1)S(1)} fusion(bf16[48,32,32]{1,2,0:T(8,128)(2,1)S(1)} %copy.29, bf16[1024,48,32]{0,2,1:T(8,128)(2,1)} %reshape.56), kind=kOutput, calls=%fused_computation.25 | convolution fusion | flops 102236160 | bytes 6389760 | tf_op jit(solution)/shard_map/ngc,gcd->ngd/dot_general | solution.py:34
  89.7 1.1 fusion.15
  90.8 0.8 copy-done.4
  91.6 5.6 %fusion.12 = (f32[1024,16,32]{0,2,1:T(8,128)}, f32[16,32]{1,0:T(8,128)S(1)}, f32[16,32]{1,0:T(8,128)S(1)}, f32[1024,16,32]{0,2,1:T(8,128)}) fusion(bf16[1024,16,3,32]{0,3,2,1:T(8,128)(2,1)S(1)} %bitcast.78, bf16[1024,16,3,32]{0,3,2,1:T(8,128)(2,1)S(1)} %bitcast.80), kind=kLoop, calls=%fused_computation.33 | loop fusion | flops 13630464 | bytes 8392704 | tf_op jit(solution)/shard_map/add | solution.py:23
  97.2 0.8 pad_maximum_fusion.8
  98.0 0.0 all-reduce.2.cloned.1.call-update
  98.1 53.2 %psum.15 = f32[32,32]{1,0:T(8,128)S(1)} all-reduce(f32[32,32]{1,0:T(8,128)S(1)} %pad_maximum_fusion.12), channel_id=1, replica_groups=mesh['groups'=2,'rows'=4,'cols'=4] {'rows','cols'}, use_global_device_ids=true, to_apply=%region_3.4 | all-reduce | flops 1024 | bytes 8192 | tf_op jit(solution)/shard_map/psum | solution.py:60
  151.3 4.3 %fusion.1 = f32[32,1,1024]{2,1,0:T(1,128)S(1)} fusion(f32[32,32,1]{1,2,0:T(1,128)S(1)} %bitcast.84, f32[1024,16,32]{0,2,1:T(8,128)} %get-tuple-element.41, f32[1024,16,32]{0,2,1:T(8,128)} %get-tuple-element.34), kind=kOutput, calls=%fused_computation.19 | convolution fusion | flops 13631488 | bytes 4329472 | tf_op jit(solution)/shard_map/nhd,hd->nh/dot_general | solution.py:75
  155.6 32.5 %all-reduce.2.cloned.1.call-done = f32[32,32,32]{2,1,0:T(8,128)} async-done(((f32[32,32,32]{2,1,0:T(8,128)}), f32[32,32,32]{2,1,0:T(8,128)}) %all-reduce.2.cloned.1.call-update) | async-done | bytes 131088 | tf_op jit(solution)/shard_map/psum | solution.py:60
  188.1 5.7 %fusion = bf16[1024,32,32]{0,2,1:T(8,128)(2,1)S(1)} fusion(f32[1024,32]{0,1:T(8,128)S(1)} %bitcast.83, f32[32,32,32]{2,1,0:T(8,128)} %all-reduce.2.cloned.1.call-done, f32[1024,16,32]{0,2,1:T(8,128)} %get-tuple-element.41, f32[1024,16,32]{0,2,1:T(8,128)} %get-tuple-element.34), kind=kOutput, calls=%fused_computation.13 | convolution fusion | flops 405798912 | bytes 6553600 | tf_op jit(solution)/shard_map/nhd,hde->nhe/dot_general | solution.py:74
  193.9 2.3 %add_convert_fusion.1 = bf16[1024,512]{1,0:T(8,128)(2,1)} fusion(bf16[1024,512]{1,0:T(8,128)(2,1)S(1)} %bitcast.86, bf16[1024,1024]{0,1:T(8,128)(2,1)S(1)} %bitcast.87, bf16[1024,512]{1,0:T(8,128)(2,1)S(1)} %copy-done.22, f32[512]{0:T(512)S(1)} %copy-done.23, f32[512]{0:T(512)S(1)} %copy-done.24), kind=kOutput, calls=%fused_computation.36 | convolution fusion | flops 1076363264 | bytes 5246976 | tf_op jit(solution)/shard_map/dot_general | solution.py:79
  (51 shorter events, 0.1 us)
Async XLA Ops:
  6.5 1.4 copy-start
  6.5 181.5 %all-reduce.2.cloned.1.call-start = ((), (), s32[]{:S(2)}) async-start(), calls=%async_computation | async-start | bytes 1048576 | tf_op jit(solution)/shard_map/psum | solution.py:60
  11.0 1.7 copy-start.1
  12.7 13.6 %collective-permute-start = (bf16[2,64,1536]{2,1,0:T(8,128)(2,1)S(1)}, bf16[2,64,1536]{2,1,0:T(8,128)(2,1)S(1)}, u32[]{:S(2)}, u32[]{:S(2)}) collective-permute-start(bf16[2,64,1536]{2,1,0:T(8,128)(2,1)S(1)} %bitcast.82), channel_id=1, source_target_pairs={{0,4},{4,8},{8,12},{1,5},{5,9},{9,13},{2,6},{6,10},{10,14},{3,7},{... | collective-permute-start | bytes 1179656 | tf_op jit(solution)/shard_map/ppermute | solution.py:16
  16.7 11.6 %collective-permute-start.1 = (bf16[2,64,1536]{2,1,0:T(8,128)(2,1)S(1)}, bf16[2,64,1536]{2,1,0:T(8,128)(2,1)S(1)}, u32[]{:S(2)}, u32[]{:S(2)}) collective-permute-start(bf16[2,64,1536]{2,1,0:T(8,128)(2,1)S(1)} %bitcast.81), channel_id=1, source_target_pairs={{4,0},{8,4},{12,8},{5,1},{9,5},{13,9},{6,2},{10,6},{14,10},{7,3},{... | collective-permute-start | bytes 1179656 | tf_op jit(solution)/shard_map/ppermute | solution.py:17
  22.8 5.5 %copy-start.2 = (bf16[1024,1536]{1,0:T(8,128)(2,1)S(1)}, bf16[1024,1536]{1,0:T(8,128)(2,1)}, u32[]{:S(2)}) copy-start(bf16[1024,1536]{1,0:T(8,128)(2,1)} %copy-done.1) | copy-start | bytes 9437188
  22.8 12.7 %copy-start.7 = (f32[25,1536]{1,0:T(8,128)S(1)}, f32[25,1536]{1,0:T(8,128)}, u32[]{:S(2)}) copy-start(f32[25,1536]{1,0:T(8,128)} %param.9) | copy-start | bytes 460804
  22.8 13.6 %copy-start.5 = (bf16[48,32,32]{0,2,1:T(8,128)(2,1)S(1)}, bf16[48,32,32]{0,2,1:T(8,128)(2,1)}, u32[]{:S(2)}) copy-start(bf16[48,32,32]{0,2,1:T(8,128)(2,1)} %param.10) | copy-start | bytes 294916
  28.5 9.8 %collective-permute-start.2 = (bf16[20,2,1536]{2,1,0:T(2,128)(2,1)S(1)}, bf16[20,2,1536]{2,1,0:T(2,128)(2,1)S(1)}, u32[]{:S(2)}, u32[]{:S(2)}) collective-permute-start(bf16[20,2,1536]{2,1,0:T(2,128)(2,1)S(1)} %get-tuple-element.32), channel_id=1, source_target_pairs={{0,1},{1,2},{2,3},{4,5},{5,6},{6,7},{8,9},{9,10},{10,11},{12,13},{... | collective-permute-start | bytes 368648 | tf_op jit(solution)/shard_map/ppermute | solution.py:16
  33.4 6.2 %collective-permute-start.3 = (bf16[20,2,1536]{2,1,0:T(2,128)(2,1)S(1)}, bf16[20,2,1536]{2,1,0:T(2,128)(2,1)S(1)}, u32[]{:S(2)}, u32[]{:S(2)}) collective-permute-start(bf16[20,2,1536]{2,1,0:T(2,128)(2,1)S(1)} %get-tuple-element.33), channel_id=1, source_target_pairs={{1,0},{2,1},{3,2},{5,4},{6,5},{7,6},{9,8},{10,9},{11,10},{13,12},{... | collective-permute-start | bytes 368648 | tf_op jit(solution)/shard_map/ppermute | solution.py:17
  38.2 6.5 %copy-start.3 = (bf16[1024,1536]{1,0:T(8,128)(2,1)S(1)}, bf16[1024,1536]{1,0:T(8,128)(2,1)}, u32[]{:S(2)}) copy-start(bf16[1024,1536]{1,0:T(8,128)(2,1)} %copy-done.1) | copy-start | bytes 9437188
  38.2 6.5 %copy-start.8 = (f32[1536]{0:T(1024)S(1)}, f32[1536]{0:T(1024)}, u32[]{:S(2)}) copy-start(f32[1536]{0:T(1024)} %get-tuple-element.11) | copy-start | bytes 18436
  38.2 6.5 %copy-start.9 = (f32[1536]{0:T(1024)S(1)}, f32[1536]{0:T(1024)}, u32[]{:S(2)}) copy-start(f32[1536]{0:T(1024)} %get-tuple-element.12) | copy-start | bytes 18436
  38.2 6.5 %copy-start.10 = (f32[1536]{0:T(1024)S(1)}, f32[1536]{0:T(1024)}, u32[]{:S(2)}) copy-start(f32[1536]{0:T(1024)} %get-tuple-element.13) | copy-start | bytes 18436
  38.2 6.5 %copy-start.11 = (f32[1536]{0:T(1024)S(1)}, f32[1536]{0:T(1024)}, u32[]{:S(2)}) copy-start(f32[1536]{0:T(1024)} %get-tuple-element.14) | copy-start | bytes 18436
  38.2 6.5 %copy-start.12 = (f32[1536]{0:T(1024)S(1)}, f32[1536]{0:T(1024)}, u32[]{:S(2)}) copy-start(f32[1536]{0:T(1024)} %get-tuple-element.15) | copy-start | bytes 18436
  38.2 6.5 %copy-start.13 = (f32[1536]{0:T(1024)S(1)}, f32[1536]{0:T(1024)}, u32[]{:S(2)}) copy-start(f32[1536]{0:T(1024)} %get-tuple-element.16) | copy-start | bytes 18436
  38.3 6.5 %copy-start.14 = (f32[1536]{0:T(1024)S(1)}, f32[1536]{0:T(1024)}, u32[]{:S(2)}) copy-start(f32[1536]{0:T(1024)} %get-tuple-element.17) | copy-start | bytes 18436
  38.3 6.5 %copy-start.15 = (f32[1536]{0:T(1024)S(1)}, f32[1536]{0:T(1024)}, u32[]{:S(2)}) copy-start(f32[1536]{0:T(1024)} %get-tuple-element.18) | copy-start | bytes 18436
  38.3 6.5 %copy-start.16 = (f32[1536]{0:T(1024)S(1)}, f32[1536]{0:T(1024)}, u32[]{:S(2)}) copy-start(f32[1536]{0:T(1024)} %get-tuple-element.19) | copy-start | bytes 18436
  38.3 6.5 %copy-start.17 = (f32[1536]{0:T(1024)S(1)}, f32[1536]{0:T(1024)}, u32[]{:S(2)}) copy-start(f32[1536]{0:T(1024)} %get-tuple-element.20) | copy-start | bytes 18436
  38.3 6.5 %copy-start.18 = (f32[1536]{0:T(1024)S(1)}, f32[1536]{0:T(1024)}, u32[]{:S(2)}) copy-start(f32[1536]{0:T(1024)} %get-tuple-element.21) | copy-start | bytes 18436
  38.3 6.5 %copy-start.19 = (f32[1536]{0:T(1024)S(1)}, f32[1536]{0:T(1024)}, u32[]{:S(2)}) copy-start(f32[1536]{0:T(1024)} %get-tuple-element.22) | copy-start | bytes 18436
  38.3 6.5 %copy-start.20 = (f32[1536]{0:T(1024)S(1)}, f32[1536]{0:T(1024)}, u32[]{:S(2)}) copy-start(f32[1536]{0:T(1024)} %get-tuple-element.23) | copy-start | bytes 18436
  89.7 1.9 copy-start.4
  91.6 5.6 %copy-start.6 = (f32[16,32,32]{2,1,0:T(8,128)S(1)}, f32[16,32,32]{2,1,0:T(8,128)}, u32[]{:S(2)}) copy-start(f32[16,32,32]{2,1,0:T(8,128)} %fusion.16) | copy-start | bytes 196612
  188.1 5.8 %copy-start.21 = (bf16[16,64,512]{2,1,0:T(8,128)(2,1)S(1)}, bf16[16,64,512]{2,1,0:T(8,128)(2,1)}, u32[]{:S(2)}) copy-start(bf16[16,64,512]{2,1,0:T(8,128)(2,1)} %param.7) | copy-start | bytes 3145732
  188.1 5.8 %copy-start.22 = (bf16[1024,512]{1,0:T(8,128)(2,1)S(1)}, bf16[1024,512]{1,0:T(8,128)(2,1)}, u32[]{:S(2)}) copy-start(bf16[1024,512]{1,0:T(8,128)(2,1)} %param.11) | copy-start | bytes 3145732
  188.1 5.8 %copy-start.23 = (f32[512]{0:T(512)S(1)}, f32[512]{0:T(512)}, u32[]{:S(2)}) copy-start(f32[512]{0:T(512)} %param.13) | copy-start | bytes 6148
  188.1 5.8 %copy-start.24 = (f32[512]{0:T(512)S(1)}, f32[512]{0:T(512)}, u32[]{:S(2)}) copy-start(f32[512]{0:T(512)} %param.12) | copy-start | bytes 6148
Sparse Core Ops, SparseCore 0:
  98.2 89.8 all-reduce.1
where the time goes:
time: 204 us; the launch traced here: 203 us
  blocking collectives  53.2 us (26%)
  waiting for transfers between devices  35.8 us (18%)
  other arithmetic  35.8 us (18%)
  local copies, waits for them, and re-layouts  29.4 us (14%)
  matrix products  22.8 us (11%)
  between operations  13.8 us (7%)
  starting transfers between devices  12.3 us (6%)
    psum x1, blocking collectives, body(): lax.psum((jnp.concatenate([plain_state, scaled_state], 0), jnp.concatenat...  53.2 us
    psum x1, waiting for transfers between devices, body(): lax.psum((jnp.concatenate([plain_state, scaled_state], 0), jnp.concatenat...  32.5 us
    convert_element_type x1, other arithmetic, aggregate(): summed.astype(jnp.bfloat16)  24 us
    reshape x1, local copies, waits for them, and re-layouts, aggregate(): summed.astype(jnp.bfloat16)  9.4 us
    ppermute x2, starting transfers between devices, padded_2(): before = lax.ppermute(last, axis, up)  8.92 us
    convert_element_type x1, local copies, waits for them, and re-layouts, aggregate(): summed.astype(jnp.bfloat16)  8.57 us
    dot_general x1, matrix products, body(): jnp.einsum('nhd,hde->nhe', queries, states, precision=lax.Precision.HIGHEST)  5.75 us
    add x1, other arithmetic, feature_map(): return jax.nn.elu(inputs.astype(jnp.float32)) + 1.0  5.57 us
  transfers between devices with their start and end apart: 5, of which 3 were waited for; matrix products, arithmetic and copies ran while one was open for 8% of the time, Pallas kernels for 0%

commit v1 on v0

--- a/solution.py
+++ b/solution.py
@@ -58,11 +58,14 @@
     aggregated = aggregate(padded, depth_kernel, group_kernel, height, breadth)
     scaled_state, scaled_total = context_states(aggregated)
     states, totals = lax.psum(
-        (
-            jnp.concatenate([plain_state, scaled_state], 0),
-            jnp.concatenate([plain_total, scaled_total], 0),
+        lax.psum(
+            (
+                jnp.concatenate([plain_state, scaled_state], 0),
+                jnp.concatenate([plain_total, scaled_total], 0),
+            ),
+            "cols",
         ),
-        ("rows", "cols"),
+        "rows",
     )
     queries = jnp.concatenate(
         [

time: 204 us -> 188 us (0.922)
  blocking collectives: 53.2 us -> 23.3 us
  waiting for transfers between devices: 35.8 us -> 47.8 us
    psum x1, blocking collectives: 53.2 us -> 9.47 us  [body(): lax.psum((jnp.concatenate([plain_state, scaled_state], 0), jnp.concatenat...]
    psum x0 -> x1, waiting for transfers between devices: none -> 36.8 us  [body(): lax.psum(lax.psum((jnp.concatenate([plain_state, scaled_state], 0), jnp.c...]
    psum x1, waiting for transfers between devices: 32.5 us -> 7.72 us  [body(): lax.psum((jnp.concatenate([plain_state, scaled_state], 0), jnp.concatenat...]
    psum x0 -> x1, blocking collectives: none -> 13.8 us  [body(): lax.psum(lax.psum((jnp.concatenate([plain_state, scaled_state], 0), jnp.c...]
  transfers between devices with their start and end apart: 5 -> 6, of which waited for: 3 -> 4; matrix products, arithmetic and copies ran while one was open for 8% -> 8% of each run, Pallas kernels for 0% -> 0%
where the time goes in v1:
time: 188 us; the launch traced here: 185 us
  waiting for transfers between devices  47.8 us (25%)
  other arithmetic  35.8 us (19%)
  local copies, waits for them, and re-layouts  29.4 us (16%)
  blocking collectives  23.3 us (12%)
  matrix products  22.8 us (12%)
  between operations  13.8 us (7%)
  starting transfers between devices  12.4 us (7%)
    psum x1, waiting for transfers between devices, body(): lax.psum(lax.psum((jnp.concatenate([plain_state, scaled_state], 0), jnp.c...  36.8 us
    convert_element_type x1, other arithmetic, aggregate(): summed.astype(jnp.bfloat16)  24 us
    psum x1, blocking collectives, body(): lax.psum(lax.psum((jnp.concatenate([plain_state, scaled_state], 0), jnp.c...  13.8 us
    psum x1, blocking collectives, body(): lax.psum((jnp.concatenate([plain_state, scaled_state], 0), jnp.concatenat...  9.47 us
    reshape x1, local copies, waits for them, and re-layouts, aggregate(): summed.astype(jnp.bfloat16)  9.4 us
    ppermute x2, starting transfers between devices, padded_2(): before = lax.ppermute(last, axis, up)  8.92 us
    convert_element_type x1, local copies, waits for them, and re-layouts, aggregate(): summed.astype(jnp.bfloat16)  8.57 us
    psum x1, waiting for transfers between devices, body(): lax.psum((jnp.concatenate([plain_state, scaled_state], 0), jnp.concatenat...  7.72 us
  transfers between devices with their start and end apart: 6, of which 4 were waited for; matrix products, arithmetic and copies ran while one was open for 8% of the time, Pallas kernels for 0%

profile of v1, /device:TPU:1, one launch (start us, length us, event | category | flops | bytes accessed | tf_op | source)
XLA Modules:
  0.0 185.2 jit_solution(4748742970227432566)
XLA Ops:
  6.5 1.4 copy-done
  7.9 3.0 %convolution_convert_fusion = bf16[1024,1536]{1,0:T(8,128)(2,1)S(1)} fusion(bf16[1024,512]{1,0:T(8,128)(2,1)} %bitcast.85, bf16[512,1536]{1,0:T(8,128)(2,1)S(1)} %copy-done), kind=kOutput, calls=%fused_computation.14 | convolution fusion | flops 1612185600 | bytes 5767168 | tf_op jit(solution)/shard_map/dot_general | solution.py:51
  11.0 1.7 copy-done.1
  12.6 0.1 fusion.25
  12.7 4.1 %collective-permute-start = (bf16[2,64,1536]{2,1,0:T(8,128)(2,1)S(1)}, bf16[2,64,1536]{2,1,0:T(8,128)(2,1)S(1)}, u32[]{:S(2)}, u32[]{:S(2)}) collective-permute-start(bf16[2,64,1536]{2,1,0:T(8,128)(2,1)S(1)} %bitcast.82), channel_id=1, source_target_pairs={{0,4},{4,8},{8,12},{1,5},{5,9},{9,13},{2,6},{6,10},{10,14},{3,7},{... | collective-permute-start | bytes 1179656 | tf_op jit(solution)/shard_map/ppermute | solution.py:16
  16.7 1.3 collective-permute-start.1
  18.0 4.7 %copy.26 = bf16[1024,1536]{0,1:T(8,128)(2,1)} copy(bf16[1024,1536]{1,0:T(8,128)(2,1)} %copy-done.1) | data formatting | bytes 6291456 | tf_op jit(solution)/shard_map/convert_element_type | solution.py:54
  22.8 3.5 %fusion.16 = f32[16,32,32]{2,1,0:T(8,128)} fusion(bf16[1024,16,3,32]{0,3,2,1:T(8,128)(2,1)} %bitcast.77), kind=kOutput, calls=%fused_computation.45 | convolution fusion | flops 36700160 | bytes 2162688 | tf_op jit(solution)/shard_map/nhd,nhe->hde/dot_general | solution.py:43
  26.3 2.0 %collective-permute-done.1 = bf16[2,64,1536]{2,1,0:T(8,128)(2,1)S(1)} collective-permute-done((bf16[2,64,1536]{2,1,0:T(8,128)(2,1)S(1)}, bf16[2,64,1536]{2,1,0:T(8,128)(2,1)S(1)}, u32[]{:S(2)}, u32[]{:S(2)}) %collective-permute-start.1) | collective-permute-done | bytes 393248 | tf_op jit(solution)/shard_map/ppermute | solution.py:17
  28.3 0.2 pad_maximum_fusion.11
  28.5 4.9 %collective-permute-start.2 = (bf16[20,2,1536]{2,1,0:T(2,128)(2,1)S(1)}, bf16[20,2,1536]{2,1,0:T(2,128)(2,1)S(1)}, u32[]{:S(2)}, u32[]{:S(2)}) collective-permute-start(bf16[20,2,1536]{2,1,0:T(2,128)(2,1)S(1)} %get-tuple-element.32), channel_id=1, source_target_pairs={{0,1},{1,2},{2,3},{4,5},{5,6},{6,7},{8,9},{9,10},{10,11},{12,13},{... | collective-permute-start | bytes 368648 | tf_op jit(solution)/shard_map/ppermute | solution.py:16
  33.4 2.1 %collective-permute-start.3 = (bf16[20,2,1536]{2,1,0:T(2,128)(2,1)S(1)}, bf16[20,2,1536]{2,1,0:T(2,128)(2,1)S(1)}, u32[]{:S(2)}, u32[]{:S(2)}) collective-permute-start(bf16[20,2,1536]{2,1,0:T(2,128)(2,1)S(1)} %get-tuple-element.33), channel_id=1, source_target_pairs={{1,0},{2,1},{3,2},{5,4},{6,5},{7,6},{9,8},{10,9},{11,10},{13,12},{... | collective-permute-start | bytes 368648 | tf_op jit(solution)/shard_map/ppermute | solution.py:17
  35.5 0.9 slice_reduce_fusion.24
  36.4 0.7 copy.29
  37.1 1.1 slice_reduce_fusion.23
  38.4 1.2 collective-permute-done.3
  39.6 5.1 %maximum_maximum_fusion = (bf16[20,66,1536]{2,1,0:T(8,128)(2,1)S(1)}, bf16[20,66,1536]{2,1,0:T(8,128)(2,1)S(1)}) fusion(bf16[2,64,1536]{2,1,0:T(8,128)(2,1)S(1)} %collective-permute-done.1, bf16[16,64,1536]{2,1,0:T(8,128)(2,1)} %bitcast.74, bf16[2,64,1536]{2,1,0:T(8,128)(2,1)S(1)} %collective-permute-done, ...), kind=kLoop, calls=%fused_computation.9 | loop fusion | flops 32440320 | bytes 12288000 | tf_op jit(solution)/shard_map/concatenate | solution.py:18
  44.9 24.0 %add_convert_fusion = bf16[16,64,1536]{2,1,0:T(8,128)(2,1)} fusion(bf16[16,64,1536]{2,1,0:T(8,128)(2,1)S(1)} %bitcast.76, bf16[2,64,1536]{2,1,0:T(8,128)(2,1)S(1)} %collective-permute-done.1, bf16[2,64,1536]{2,1,0:T(8,128)(2,1)S(1)} %collective-permute-done, bf16[20,66,1536]{2,1,0:T(8,128)(2,1)S(1)} %get-tuple-element.31, ...), kind=kLoop, calls=%fused_computation.8 | loop fusion | flops 124256256 | bytes 70146048 | tf_op jit(solution)/shard_map/convert_element_type | solution.py:33
  68.9 8.6 %copy.28 = bf16[16,64,1536]{1,0,2:T(8,128)(2,1)} copy(bf16[16,64,1536]{2,1,0:T(8,128)(2,1)} %add_convert_fusion) | data formatting | bytes 6291456 | tf_op jit(solution)/shard_map/convert_element_type | solution.py:33
  77.5 9.4 %reshape.56 = bf16[1024,48,32]{0,2,1:T(8,128)(2,1)} reshape(bf16[16,64,1536]{1,0,2:T(8,128)(2,1)} %copy.28) | data formatting | bytes 6291456 | tf_op jit(solution)/shard_map/reshape | solution.py:33
  86.9 2.8 %convolution_convert_fusion.1 = bf16[48,1024,32]{1,2,0:T(8,128)(2,1)S(1)} fusion(bf16[48,32,32]{1,2,0:T(8,128)(2,1)S(1)} %copy.29, bf16[1024,48,32]{0,2,1:T(8,128)(2,1)} %reshape.56), kind=kOutput, calls=%fused_computation.25 | convolution fusion | flops 102236160 | bytes 6389760 | tf_op jit(solution)/shard_map/ngc,gcd->ngd/dot_general | solution.py:34
  89.7 1.1 fusion.15
  90.8 0.8 copy-done.4
  91.6 5.6 %fusion.12 = (f32[1024,16,32]{0,2,1:T(8,128)}, f32[16,32]{1,0:T(8,128)S(1)}, f32[16,32]{1,0:T(8,128)S(1)}, f32[1024,16,32]{0,2,1:T(8,128)}) fusion(bf16[1024,16,3,32]{0,3,2,1:T(8,128)(2,1)S(1)} %bitcast.78, bf16[1024,16,3,32]{0,3,2,1:T(8,128)(2,1)S(1)} %bitcast.80), kind=kLoop, calls=%fused_computation.33 | loop fusion | flops 13630464 | bytes 8392704 | tf_op jit(solution)/shard_map/add | solution.py:23
  97.2 0.8 pad_maximum_fusion.8
  98.1 9.5 %psum.30 = f32[32,32]{1,0:T(8,128)S(1)} all-reduce(f32[32,32]{1,0:T(8,128)S(1)} %pad_maximum_fusion.12), channel_id=1, replica_groups=mesh['groups'=2,'rows'=4,'cols'=4] {'cols'}, use_global_device_ids=true, to_apply=%region_4.5 | all-reduce | flops 1024 | bytes 8192 | tf_op jit(solution)/shard_map/psum | solution.py:61
  107.6 13.8 %psum.31 = f32[32,32]{1,0:T(8,128)S(1)} all-reduce(f32[32,32]{1,0:T(8,128)S(1)} %psum.30), channel_id=1, replica_groups=mesh['groups'=2,'rows'=4,'cols'=4] {'rows'}, use_global_device_ids=true, to_apply=%region_5.6 | all-reduce | flops 1024 | bytes 8192 | tf_op jit(solution)/shard_map/psum | solution.py:60
  121.4 7.7 %all-reduce.3.cloned.1.call-done = f32[32,32,32]{2,1,0:T(8,128)} async-done(((f32[32,32,32]{2,1,0:T(8,128)}), f32[32,32,32]{2,1,0:T(8,128)}) %all-reduce.3.cloned.1.call-update) | async-done | bytes 131088 | tf_op jit(solution)/shard_map/psum | solution.py:61
  129.1 4.3 %fusion.1 = f32[32,1,1024]{2,1,0:T(1,128)S(1)} fusion(f32[32,32,1]{1,2,0:T(1,128)S(1)} %bitcast.84, f32[1024,16,32]{0,2,1:T(8,128)} %get-tuple-element.41, f32[1024,16,32]{0,2,1:T(8,128)} %get-tuple-element.34), kind=kOutput, calls=%fused_computation.19 | convolution fusion | flops 13631488 | bytes 4329472 | tf_op jit(solution)/shard_map/nhd,hd->nh/dot_general | solution.py:78
  133.5 36.8 %all-reduce.5.cloned.1.call-done = f32[32,32,32]{2,1,0:T(8,128)} async-done(((f32[32,32,32]{2,1,0:T(8,128)}), f32[32,32,32]{2,1,0:T(8,128)}) %all-reduce.5.cloned.1.call-update) | async-done | bytes 131088 | tf_op jit(solution)/shard_map/psum | solution.py:60
  170.3 5.7 %fusion = bf16[1024,32,32]{0,2,1:T(8,128)(2,1)S(1)} fusion(f32[1024,32]{0,1:T(8,128)S(1)} %bitcast.83, f32[32,32,32]{2,1,0:T(8,128)} %all-reduce.5.cloned.1.call-done, f32[1024,16,32]{0,2,1:T(8,128)} %get-tuple-element.41, f32[1024,16,32]{0,2,1:T(8,128)} %get-tuple-element.34), kind=kOutput, calls=%fused_computation.13 | convolution fusion | flops 405798912 | bytes 6553600 | tf_op jit(solution)/shard_map/nhd,hde->nhe/dot_general | solution.py:77
  176.1 2.3 %add_convert_fusion.1 = bf16[1024,512]{1,0:T(8,128)(2,1)} fusion(bf16[1024,512]{1,0:T(8,128)(2,1)S(1)} %bitcast.86, bf16[1024,1024]{0,1:T(8,128)(2,1)S(1)} %bitcast.87, bf16[1024,512]{1,0:T(8,128)(2,1)S(1)} %copy-done.22, f32[512]{0:T(512)S(1)} %copy-done.23, f32[512]{0:T(512)S(1)} %copy-done.24), kind=kOutput, calls=%fused_computation.36 | convolution fusion | flops 1076363264 | bytes 5246976 | tf_op jit(solution)/shard_map/dot_general | solution.py:82
  (55 shorter events, 0.2 us)
Async XLA Ops:
  6.5 1.4 copy-start
  6.5 122.6 %all-reduce.3.cloned.1.call-start = ((), (), s32[]{:S(2)}) async-start(), calls=%async_computation | async-start | bytes 1048576 | tf_op jit(solution)/shard_map/psum | solution.py:61
  11.0 1.7 copy-start.1
  12.7 13.6 %collective-permute-start = (bf16[2,64,1536]{2,1,0:T(8,128)(2,1)S(1)}, bf16[2,64,1536]{2,1,0:T(8,128)(2,1)S(1)}, u32[]{:S(2)}, u32[]{:S(2)}) collective-permute-start(bf16[2,64,1536]{2,1,0:T(8,128)(2,1)S(1)} %bitcast.82), channel_id=1, source_target_pairs={{0,4},{4,8},{8,12},{1,5},{5,9},{9,13},{2,6},{6,10},{10,14},{3,7},{... | collective-permute-start | bytes 1179656 | tf_op jit(solution)/shard_map/ppermute | solution.py:16
  16.7 11.6 %collective-permute-start.1 = (bf16[2,64,1536]{2,1,0:T(8,128)(2,1)S(1)}, bf16[2,64,1536]{2,1,0:T(8,128)(2,1)S(1)}, u32[]{:S(2)}, u32[]{:S(2)}) collective-permute-start(bf16[2,64,1536]{2,1,0:T(8,128)(2,1)S(1)} %bitcast.81), channel_id=1, source_target_pairs={{4,0},{8,4},{12,8},{5,1},{9,5},{13,9},{6,2},{10,6},{14,10},{7,3},{... | collective-permute-start | bytes 1179656 | tf_op jit(solution)/shard_map/ppermute | solution.py:17
  22.8 5.5 %copy-start.2 = (bf16[1024,1536]{1,0:T(8,128)(2,1)S(1)}, bf16[1024,1536]{1,0:T(8,128)(2,1)}, u32[]{:S(2)}) copy-start(bf16[1024,1536]{1,0:T(8,128)(2,1)} %copy-done.1) | copy-start | bytes 9437188
  22.8 12.7 %copy-start.7 = (f32[25,1536]{1,0:T(8,128)S(1)}, f32[25,1536]{1,0:T(8,128)}, u32[]{:S(2)}) copy-start(f32[25,1536]{1,0:T(8,128)} %param.9) | copy-start | bytes 460804
  22.8 13.6 %copy-start.5 = (bf16[48,32,32]{0,2,1:T(8,128)(2,1)S(1)}, bf16[48,32,32]{0,2,1:T(8,128)(2,1)}, u32[]{:S(2)}) copy-start(bf16[48,32,32]{0,2,1:T(8,128)(2,1)} %param.10) | copy-start | bytes 294916
  28.5 9.8 %collective-permute-start.2 = (bf16[20,2,1536]{2,1,0:T(2,128)(2,1)S(1)}, bf16[20,2,1536]{2,1,0:T(2,128)(2,1)S(1)}, u32[]{:S(2)}, u32[]{:S(2)}) collective-permute-start(bf16[20,2,1536]{2,1,0:T(2,128)(2,1)S(1)} %get-tuple-element.32), channel_id=1, source_target_pairs={{0,1},{1,2},{2,3},{4,5},{5,6},{6,7},{8,9},{9,10},{10,11},{12,13},{... | collective-permute-start | bytes 368648 | tf_op jit(solution)/shard_map/ppermute | solution.py:16
  33.4 6.2 %collective-permute-start.3 = (bf16[20,2,1536]{2,1,0:T(2,128)(2,1)S(1)}, bf16[20,2,1536]{2,1,0:T(2,128)(2,1)S(1)}, u32[]{:S(2)}, u32[]{:S(2)}) collective-permute-start(bf16[20,2,1536]{2,1,0:T(2,128)(2,1)S(1)} %get-tuple-element.33), channel_id=1, source_target_pairs={{1,0},{2,1},{3,2},{5,4},{6,5},{7,6},{9,8},{10,9},{11,10},{13,12},{... | collective-permute-start | bytes 368648 | tf_op jit(solution)/shard_map/ppermute | solution.py:17
  38.2 6.5 %copy-start.3 = (bf16[1024,1536]{1,0:T(8,128)(2,1)S(1)}, bf16[1024,1536]{1,0:T(8,128)(2,1)}, u32[]{:S(2)}) copy-start(bf16[1024,1536]{1,0:T(8,128)(2,1)} %copy-done.1) | copy-start | bytes 9437188
  38.2 6.5 %copy-start.8 = (f32[1536]{0:T(1024)S(1)}, f32[1536]{0:T(1024)}, u32[]{:S(2)}) copy-start(f32[1536]{0:T(1024)} %get-tuple-element.11) | copy-start | bytes 18436
  38.2 6.5 %copy-start.9 = (f32[1536]{0:T(1024)S(1)}, f32[1536]{0:T(1024)}, u32[]{:S(2)}) copy-start(f32[1536]{0:T(1024)} %get-tuple-element.12) | copy-start | bytes 18436
  38.2 6.5 %copy-start.10 = (f32[1536]{0:T(1024)S(1)}, f32[1536]{0:T(1024)}, u32[]{:S(2)}) copy-start(f32[1536]{0:T(1024)} %get-tuple-element.13) | copy-start | bytes 18436
  38.2 6.5 %copy-start.11 = (f32[1536]{0:T(1024)S(1)}, f32[1536]{0:T(1024)}, u32[]{:S(2)}) copy-start(f32[1536]{0:T(1024)} %get-tuple-element.14) | copy-start | bytes 18436
  38.3 6.5 %copy-start.12 = (f32[1536]{0:T(1024)S(1)}, f32[1536]{0:T(1024)}, u32[]{:S(2)}) copy-start(f32[1536]{0:T(1024)} %get-tuple-element.15) | copy-start | bytes 18436
  38.3 6.5 %copy-start.13 = (f32[1536]{0:T(1024)S(1)}, f32[1536]{0:T(1024)}, u32[]{:S(2)}) copy-start(f32[1536]{0:T(1024)} %get-tuple-element.16) | copy-start | bytes 18436
  38.3 6.5 %copy-start.14 = (f32[1536]{0:T(1024)S(1)}, f32[1536]{0:T(1024)}, u32[]{:S(2)}) copy-start(f32[1536]{0:T(1024)} %get-tuple-element.17) | copy-start | bytes 18436
  38.3 6.5 %copy-start.15 = (f32[1536]{0:T(1024)S(1)}, f32[1536]{0:T(1024)}, u32[]{:S(2)}) copy-start(f32[1536]{0:T(1024)} %get-tuple-element.18) | copy-start | bytes 18436
  38.3 6.5 %copy-start.16 = (f32[1536]{0:T(1024)S(1)}, f32[1536]{0:T(1024)}, u32[]{:S(2)}) copy-start(f32[1536]{0:T(1024)} %get-tuple-element.19) | copy-start | bytes 18436
  38.3 6.5 %copy-start.17 = (f32[1536]{0:T(1024)S(1)}, f32[1536]{0:T(1024)}, u32[]{:S(2)}) copy-start(f32[1536]{0:T(1024)} %get-tuple-element.20) | copy-start | bytes 18436
  38.3 6.5 %copy-start.18 = (f32[1536]{0:T(1024)S(1)}, f32[1536]{0:T(1024)}, u32[]{:S(2)}) copy-start(f32[1536]{0:T(1024)} %get-tuple-element.21) | copy-start | bytes 18436
  38.3 6.5 %copy-start.19 = (f32[1536]{0:T(1024)S(1)}, f32[1536]{0:T(1024)}, u32[]{:S(2)}) copy-start(f32[1536]{0:T(1024)} %get-tuple-element.22) | copy-start | bytes 18436
  38.3 6.5 %copy-start.20 = (f32[1536]{0:T(1024)S(1)}, f32[1536]{0:T(1024)}, u32[]{:S(2)}) copy-start(f32[1536]{0:T(1024)} %get-tuple-element.23) | copy-start | bytes 18436
  89.7 1.9 %copy-start.4 = (bf16[1024,1536]{0,1:T(8,128)(2,1)S(1)}, bf16[1024,1536]{0,1:T(8,128)(2,1)}, u32[]{:S(2)}) copy-start(bf16[1024,1536]{0,1:T(8,128)(2,1)} %copy.26) | copy-start | bytes 9437188
  91.6 5.6 %copy-start.6 = (f32[16,32,32]{2,1,0:T(8,128)S(1)}, f32[16,32,32]{2,1,0:T(8,128)}, u32[]{:S(2)}) copy-start(f32[16,32,32]{2,1,0:T(8,128)} %fusion.16) | copy-start | bytes 196612
  98.0 72.2 %all-reduce.5.cloned.1.call-start = ((), (), s32[]{:S(2)}) async-start(), calls=%async_computation.1 | async-start | bytes 1048576 | tf_op jit(solution)/shard_map/psum | solution.py:60
  170.3 5.8 %copy-start.21 = (bf16[16,64,512]{2,1,0:T(8,128)(2,1)S(1)}, bf16[16,64,512]{2,1,0:T(8,128)(2,1)}, u32[]{:S(2)}) copy-start(bf16[16,64,512]{2,1,0:T(8,128)(2,1)} %param.7) | copy-start | bytes 3145732
  170.3 5.8 %copy-start.22 = (bf16[1024,512]{1,0:T(8,128)(2,1)S(1)}, bf16[1024,512]{1,0:T(8,128)(2,1)}, u32[]{:S(2)}) copy-start(bf16[1024,512]{1,0:T(8,128)(2,1)} %param.11) | copy-start | bytes 3145732
  170.3 5.8 %copy-start.23 = (f32[512]{0:T(512)S(1)}, f32[512]{0:T(512)}, u32[]{:S(2)}) copy-start(f32[512]{0:T(512)} %param.13) | copy-start | bytes 6148
  170.3 5.8 %copy-start.24 = (f32[512]{0:T(512)S(1)}, f32[512]{0:T(512)}, u32[]{:S(2)}) copy-start(f32[512]{0:T(512)} %param.12) | copy-start | bytes 6148
Sparse Core Ops, SparseCore 0:
  98.2 30.8 all-reduce.2
  131.4 38.7 all-reduce.4
